TPU v7x, 32 devices: a whole 2x2x4 slice. The times are simulated.
32 devices in a mesh: gx: 2 (over x), gy: 4 (over y, core), gz: 4 (over z).
Axes of the slice: x: 2, y: 2, z: 4, core: 2. Of those that a mesh axis runs over, the one named last changes fastest.
Arguments:
- right_side: float32 [32, 64, 1024], P('gx', 'gy', 'gz'), may hold values from -5 to 5
- coefficients: float32 [4, 32, 64, 1024], P(None, 'gx', 'gy', 'gz'), may hold values from 0.1 to 32
- first_guess: float32 [32, 64, 1024], P('gx', 'gy', 'gz'), may hold values from -3 to 3
Outputs:
- solution_field: float32 [32, 64, 1024], P('gx', 'gy', 'gz')
All inputs are finite; a program needn't handle non-finite values.
Results may differ from a plain program's by a relative error of at most 0.00002.
Values sent between devices are 32-bit elements; how exact they have to be, the bound alone decides.
A program may use at most 128 MiB of HBM per device.

v0:
```python
import functools

import jax
import jax.numpy as jnp
from jax import lax
from jax.experimental import pallas as pl
from jax.experimental.pallas import tpu as pltpu
from jax.sharding import PartitionSpec as P

CYCLES = 2
SWEEPS = 8
REACH = 2 * (SWEEPS + 1)
STEP = 20
LANES = 128
CHUNK = 1

relaxation = 0.8
blending = 0.4
MESH = pl.DeviceIdType.MESH


def iota(shape, dim):
    return lax.broadcasted_iota(jnp.int32, shape, dim)


def spread(a, b):
    total = None
    for _ in range(3):
        part = a.astype(jnp.bfloat16)
        a = a - part.astype(jnp.float32)
        term = jnp.dot(part, b, preferred_element_type=jnp.float32)
        total = term if total is None else total + term
    return total


def kernel(sizes, names, b_ref, k_ref, g_ref, out_ref, *scratch):
    (fields, cells, tiles, es, yss, yrs, ms, fs, kxr, kys, kyr, zs, zr, us, ur,
     send, recv, ksend, krecv, zsend, zrecv) = scratch
    nx, ny, nz = sizes
    wide = nz + LANES
    shapes = ((nx // 2, ny, wide), (nx, ny // 2, wide), (nx, ny, nz // 2 + LANES), (nx, ny, wide))
    place = [lax.axis_index(n) for n in names]
    counts = [lax.axis_size(n) for n in names]
    has_low = [p > 0 for p in place]
    has_high = [p < c - 1 for p, c in zip(place, counts)]
    ways = []
    for axis in range(3):
        ways.append((axis, -1, has_low[axis], has_high[axis]))
        ways.append((axis, 1, has_high[axis], has_low[axis]))

    def target(way):
        axis, step = ways[way][:2]
        return {names[axis]: place[axis] + step}

    def copy(src, dst, ssem, rsem, way):
        return pltpu.make_async_remote_copy(
            src_ref=src, dst_ref=dst, send_sem=ssem, recv_sem=rsem,
            device_id=target(way), device_id_type=MESH,
        )

    def start(copies):
        for way, c in copies:
            @pl.when(ways[way][2])
            def _():
                c.start()

    def finish(copies):
        for way, c in copies:
            @pl.when(ways[way][3])
            def _():
                c.wait_recv()
        for way, c in copies:
            @pl.when(ways[way][2])
            def _():
                c.wait_send()

    def faces(g, slot, keep=(0, 1, 2, 3)):
        x = shapes[g][0]
        e, ys, yr = es[g], yss[g], yrs[g]
        ends = (
            (e.at[slot, 1], e.at[slot, x + 1]),
            (e.at[slot, x], e.at[slot, 0]),
            (ys.at[slot, 0], yr.at[slot, 1]),
            (ys.at[slot, 1], yr.at[slot, 0]),
        )
        return [
            (way, copy(*ends[way], send.at[g, way, slot], recv.at[g, way, slot], way)) for way in keep
        ]

    for g in range(4):
        x = shapes[g][0]
        for slot in range(2):
            zero = jnp.zeros(shapes[g][1:], jnp.float32)
            es[g][slot, 0] = zero
            es[g][slot, x + 1] = zero
        yrs[g][...] = jnp.zeros(yrs[g].shape, jnp.float32)
    kxr[...] = jnp.zeros(kxr.shape, jnp.float32)
    kyr[...] = jnp.zeros(kyr.shape, jnp.float32)
    zr[...] = jnp.zeros(zr.shape, jnp.float32)
    ur[...] = jnp.zeros(ur.shape, jnp.float32)

    barrier = pltpu.get_barrier_semaphore()
    for way in range(6):
        @pl.when(ways[way][2])
        def _():
            pl.semaphore_signal(barrier, inc=1, device_id=target(way), device_id_type=MESH)
    peers = sum(jnp.where(has, 1, 0) for has in has_low + has_high)
    pl.semaphore_wait(barrier, peers)

    lane = iota((nx, ny, LANES), 2)
    low = jnp.zeros((nx, ny, LANES), jnp.float32)
    high = low
    for j in range(6):
        if j < 4:
            first, last = k_ref[j, :, :, :LANES], k_ref[j, :, :, nz - LANES:]
        elif j == 4:
            first, last = g_ref[:, :, :LANES], g_ref[:, :, nz - LANES:]
        else:
            first, last = b_ref[:, :, :LANES], b_ref[:, :, nz - LANES:]
        here = (lane >= STEP * j) & (lane < STEP * j + REACH)
        low = jnp.where(here, pltpu.roll(first, STEP * j, 2) if j else first, low)
        high = jnp.where(here, pltpu.roll(last, (STEP * j + REACH) % LANES, 2), high)
    zs[0] = low
    zs[1] = high
    deep = [
        (4, copy(zs.at[0], zr.at[1], zsend.at[0], zrecv.at[0], 4)),
        (5, copy(zs.at[1], zr.at[0], zsend.at[1], zrecv.at[1], 5)),
    ]
    start(deep)
    for j in range(4):
        fields[j, :, :, :nz] = k_ref[j]
    fields[4, :, :, :nz] = b_ref[...]
    es[3][0, 1:nx + 1, :, :nz] = g_ref[...]
    finish(deep)
    above, below = zr[1], zr[0]

    def beside(j):
        up = pltpu.roll(above, (LANES - STEP * j) % LANES, 2) if j else above
        down = pltpu.roll(below, (2 * LANES - REACH - STEP * j) % LANES, 2)
        return jnp.where(lane < REACH, up, jnp.where(lane >= LANES - REACH, down, 0.0))

    for j in range(4):
        fields[j, :, :, nz:] = beside(j)
    es[3][0, 1:nx + 1, :, nz:] = beside(4)
    fields[4, :, :, nz:] = beside(5)

    def send_guess(slot):
        u = es[3][slot, 1:nx + 1]
        yss[3][slot, 0] = u[:, 0:1, :]
        yss[3][slot, 1] = u[:, ny - 1:ny, :]
        start(faces(3, slot))

    ky = fields[1]
    for row in range(2):
        kys[0, row] = ky[:, row:row + 1, :]
        kys[1, row] = ky[:, ny - 2 + row:ny - 1 + row, :]
    edges = [
        (0, copy(fields.at[0, pl.ds(0, 2)], kxr.at[1], ksend.at[0], krecv.at[0], 0)),
        (1, copy(fields.at[0, pl.ds(nx - 2, 2)], kxr.at[0], ksend.at[1], krecv.at[1], 1)),
        (2, copy(kys.at[0], kyr.at[1], ksend.at[2], krecv.at[2], 2)),
        (3, copy(kys.at[1], kyr.at[0], ksend.at[3], krecv.at[3], 3)),
    ]
    start(edges)
    send_guess(0)

    half = nz // 2
    r, c = iota((wide, half + LANES), 0), iota((wide, half + LANES), 1)
    home = jnp.where(
        r < nz, r // 2,
        jnp.where(r < nz + LANES // 2, half + (r - nz) // 2, half + LANES // 2 + (r - nz) // 2),
    )
    z_mean = jnp.where(home == c, 0.5, 0.0).astype(jnp.bfloat16)
    rows = nx * ny
    r, c = iota((half + LANES, nz), 0), iota((half + LANES, nz), 1)
    main = c // 2
    total = half + LANES
    side = jnp.where(c % 2 == 1, main + 1, jnp.where(main == 0, total - 1, main - 1))
    z_spread = (jnp.where(r == main, 0.75, 0.0) + jnp.where(r == side, 0.25, 0.0)).astype(jnp.bfloat16)

    count = wide // LANES
    even_rows, odd_rows = pl.ds(0, ny // 2, stride=2), pl.ds(1, ny // 2, stride=2)

    def put_tiles(planes, values):
        for t in range(values.shape[2] // LANES):
            tiles[t, planes] = values[:, :, LANES * t:LANES * (t + 1)]

    def get_tiles(planes, tiles_of=count):
        return jnp.concatenate([tiles[t, planes] for t in range(tiles_of)], 2)

    def y_mean(planes):
        return jnp.concatenate(
            [0.5 * (tiles[t, planes, even_rows] + tiles[t, planes, odd_rows]) for t in range(count)], 2)

    def chunks(x, step=CHUNK):
        return [slice(x0, x0 + step) for x0 in range(0, x, step)]

    def below_of(ref, planes, halo):
        if planes.start > 0:
            return ref[planes.start - 1:planes.stop - 1]
        return halo if planes.stop == 1 else jnp.concatenate([halo, ref[0:planes.stop - 1]], 0)

    def above_of(ref, planes, halo):
        if planes.stop < ref.shape[0]:
            return ref[planes.start + 1:planes.stop + 1]
        if planes.stop == planes.start + 1:
            return halo
        return jnp.concatenate([ref[planes.start + 1:planes.stop], halo], 0)

    def y_shift(values, halo_low, halo_high):
        y = values.shape[1]
        row = iota(values.shape, 1)
        lower = jnp.where(row == 0, halo_low, pltpu.roll(values, 1, 1))
        upper = jnp.where(row == y - 1, halo_high, pltpu.roll(values, y - 1, 1))
        return lower, upper

    def z_shift(values):
        return pltpu.roll(values, 1, 2), pltpu.roll(values, values.shape[2] - 1, 2)

    def face_weights(k, planes, near_x, near_y):
        k0, k1, k2 = k.at[0], k.at[1], k.at[2]
        m1, m2 = k1[planes], k2[planes]
        groups = (
            (k0[planes], (below_of(k0, planes, near_x[0]), above_of(k0, planes, near_x[1]))),
            (m1, y_shift(m1, near_y[0](planes), near_y[1](planes))),
            (m2, z_shift(m2)),
        )
        found = []
        total = k[3, planes]
        for middle, pair in groups:
            for other in pair:
                found.append(0.5 * (middle + other))
                total = total + found[-1]
        return found, total

    for j in range(4):
        for d in range(2):
            factor = 0.25 if j == d else 1.0
            if d == 0:
                for i in range(nx // 2):
                    cells[0][j, i] = (0.5 * factor) * (fields[j, 2 * i] + fields[j, 2 * i + 1])
            else:
                for planes in chunks(nx):
                    put_tiles(planes, fields[j, planes])
                for planes in chunks(nx):
                    cells[1][j, planes] = y_mean(planes) * factor
    for j in range(4):
        factor = 0.25 if j == 2 else 1.0
        for planes in chunks(nx, nx // 2):
            flat = fields[j, planes].reshape((rows // 2, wide))
            cells[2][j, planes] = (spread(flat, z_mean) * factor).reshape((nx // 2,) + shapes[2][1:])
    finish(edges)
    near_rows = [kxr[0, 1], kxr[1, 0]] + [kyr[0, 1].reshape((nx, wide)), kyr[1, 0].reshape((nx, wide))]
    edge = spread(jnp.concatenate(near_rows, 0), z_mean)
    edge_x = [edge[0:ny][None], edge[ny:2 * ny][None]]
    edge_y = [edge[2 * ny + nx * side:2 * ny + nx * (side + 1)].reshape((nx, 1, half + LANES)) for side in range(2)]
    put_tiles(slice(0, 2), jnp.stack([kxr[0, 1], kxr[1, 0]]))
    pair = y_mean(slice(0, 2))

    near_xs = (
        [0.125 * (kxr[side, 0:1] + kxr[side, 1:2]) for side in range(2)],
        [pair[0:1], pair[1:2]],
        edge_x,
    )

    def y_face(d, side):
        nearest = kyr.at[side, 1 - side]
        if d == 0:
            return lambda planes: jnp.concatenate(
                [0.5 * (nearest[2 * i:2 * i + 1] + nearest[2 * i + 1:2 * i + 2])
                 for i in range(planes.start, planes.stop)], 0)
        if d == 1:
            return lambda planes: 0.125 * (kyr[side, 0, planes] + kyr[side, 1, planes])
        if d == 2:
            return lambda planes: edge_y[side][planes]
        return lambda planes: nearest[planes]

    for d in range(3):
        for planes in chunks(shapes[d][0]):
            w, total_coarse = face_weights(
                cells[d], planes, near_xs[d], (y_face(d, 0), y_face(d, 1)))
            inside = cells[d][3, planes] > 0.0
            scale = jnp.where(inside, relaxation / jnp.where(inside, total_coarse, 1.0), 0.0)
            ms[d][6, planes] = scale
            for j in range(6):
                ms[d][j, planes] = w[j] * scale

    def sweep(g, slot, new_slot, keep=(0, 1, 2, 3)):
        e, yr, ys, m, f = es[g], yrs[g], yss[g], ms[g], fs[g]
        x, y, z = shapes[g]
        order = list(range(0, x, CHUNK))
        order = order[:1] + order[-1:] + order[1:-1]
        for x0 in order:
            planes = slice(x0, x0 + CHUNK)
            middle = e[slot, x0 + 1:x0 + 1 + CHUNK]
            y_low, y_high = y_shift(middle, yr[slot, 0, planes], yr[slot, 1, planes])
            z_low, z_high = z_shift(middle)
            new = (1.0 - relaxation) * middle + f[planes]
            new = new + m[0, planes] * e[slot, x0:x0 + CHUNK]
            new = new + m[1, planes] * e[slot, x0 + 2:x0 + 2 + CHUNK]
            new = new + m[2, planes] * y_low
            new = new + m[3, planes] * y_high
            new = new + m[4, planes] * z_low
            new = new + m[5, planes] * z_high
            e[new_slot, x0 + 1:x0 + 1 + CHUNK] = new
            ys[new_slot, 0, planes] = new[:, 0:1]
            ys[new_slot, 1, planes] = new[:, y - 1:y]
            if x0 == order[1] and 0 in keep:
                start(faces(g, new_slot, (0, 1)))
        if 2 in keep:
            start(faces(g, new_slot, (2, 3)))

    for cycle in range(CYCLES):
        slot = cycle % 2
        finish(faces(3, slot))
        u = es[3]
        for planes in chunks(nx):
            x0, x1 = planes.start, planes.stop
            middle = u[slot, x0 + 1:x1 + 1]
            y_low, y_high = y_shift(middle, yrs[3][slot, 0, planes], yrs[3][slot, 1, planes])
            z_low, z_high = z_shift(middle)
            w, total_fine = face_weights(
                fields, planes, (kxr[0, 1:2], kxr[1, 0:1]), (y_face(3, 0), y_face(3, 1)))
            residual = fields[4, planes] - total_fine * middle
            around = (u[slot, x0:x1], u[slot, x0 + 2:x1 + 2], y_low, y_high, z_low, z_high)
            for j in range(6):
                residual = residual + w[j] * around[j]
            put_tiles(planes, residual)
        for g in range(3):
            x, y, z = shapes[g]
            if g == 2:
                flat = get_tiles(slice(0, nx)).reshape((rows, wide))
                whole = spread(flat, z_mean).reshape(shapes[2])
            for planes in chunks(x):
                if g == 0:
                    pairs = [get_tiles(slice(2 * i, 2 * i + 2)) for i in range(planes.start, planes.stop)]
                    first = jnp.concatenate([0.5 * (p[0:1] + p[1:2]) for p in pairs], 0)
                elif g == 1:
                    first = y_mean(planes)
                else:
                    first = whole[planes]
                first = ms[g][6, planes] * first
                fs[g][planes] = first
                es[g][1, planes.start + 1:planes.stop + 1] = first
                yss[g][1, 0, planes] = first[:, 0:1]
                yss[g][1, 1, planes] = first[:, y - 1:y]
            start(faces(g, 1))

        @pl.loop(1, SWEEPS - 1)
        def _(repeat):
            old = lax.rem(repeat, 2)
            for g in range(3):
                finish(faces(g, old))
                sweep(g, old, 1 - old)

        last = SWEEPS % 2
        needed = ((0, 1), (2, 3), ())
        for g in range(3):
            finish(faces(g, 1 - last))
            sweep(g, 1 - last, last, needed[g])
        e = es[2][last, 1:nx + 1].reshape((rows, half + LANES))
        from_z = spread(e, z_spread).reshape((nx, ny, nz))
        finish(faces(1, last, needed[1]))
        for planes in chunks(nx):
            e = es[1][last, planes.start + 1:planes.stop + 1, :, :nz]
            y_low, y_high = y_shift(
                e, yrs[1][last, 0, planes, :, :nz], yrs[1][last, 1, planes, :, :nz])
            even = 0.75 * e + 0.25 * y_low
            odd = 0.75 * e + 0.25 * y_high
            for t in range(nz // LANES):
                tiles[t, planes, even_rows] = even[:, :, LANES * t:LANES * (t + 1)]
                tiles[t, planes, odd_rows] = odd[:, :, LANES * t:LANES * (t + 1)]
        finish(faces(0, last, needed[0]))
        for i in range(nx // 2):
            planes = slice(2 * i, 2 * i + 2)
            e = es[0][last, i:i + 3, :, :nz]
            even = 0.75 * e[1:2] + 0.25 * e[0:1]
            odd = 0.75 * e[1:2] + 0.25 * e[2:3]
            update = (jnp.concatenate([even, odd], 0) + get_tiles(planes, nz // LANES)) + from_z[planes]
            final = es[3][slot, 2 * i + 1:2 * i + 3, :, :nz] + blending * update
            if cycle == CYCLES - 1:
                out_ref[planes] = final
            else:
                es[3][1 - slot, 2 * i + 1:2 * i + 3, :, :nz] = final
        if cycle == CYCLES - 1:
            continue
        result = es[3].at[1 - slot, 1:nx + 1]
        per = LANES // STEP
        plane_lane = iota((ny, LANES), 1)
        groups = us.shape[1]
        for q in range(groups):
            low = jnp.zeros((ny, LANES), jnp.float32)
            high = low
            for p in range(min(per, nx - q * per)):
                here = (plane_lane >= STEP * p) & (plane_lane < STEP * p + REACH)
                first = result[q * per + p, :, :LANES]
                low = jnp.where(here, pltpu.roll(first, STEP * p, 1) if p else first, low)
                high = jnp.where(
                    here, pltpu.roll(result[q * per + p, :, nz - LANES:nz], (STEP * p + REACH) % LANES, 1), high)
            us[0, q] = low
            us[1, q] = high
        again = [
            (4, copy(us.at[0], ur.at[1], zsend.at[2], zrecv.at[2], 4)),
            (5, copy(us.at[1], ur.at[0], zsend.at[3], zrecv.at[3], 5)),
        ]
        start(again)
        finish(again)
        for i in range(nx):
            q, p = i // per, i % per
            up = pltpu.roll(ur[1, q], (LANES - STEP * p) % LANES, 1) if p else ur[1, q]
            down = pltpu.roll(ur[0, q], (2 * LANES - REACH - STEP * p) % LANES, 1)
            es[3][1 - slot, i + 1, :, nz:] = jnp.where(
                plane_lane < REACH, up, jnp.where(plane_lane >= LANES - REACH, down, 0.0))
        send_guess(1 - slot)


def body(names, right_side, coefficients, first_guess):
    nx, ny, nz = right_side.shape
    wide = nz + LANES
    shapes = ((nx // 2, ny, wide), (nx, ny // 2, wide), (nx, ny, nz // 2 + LANES), (nx, ny, wide))
    f32 = jnp.float32
    vmem = lambda *shape: pltpu.VMEM(shape, f32)
    dma = pltpu.SemaphoreType.DMA
    groups = -(-nx // (LANES // STEP))
    scratch = [
        vmem(5, nx, ny, wide),
        tuple(vmem(4, x, y, z) for x, y, z in shapes[:3]),
        vmem(wide // LANES, nx, ny, LANES),
        tuple(vmem(2, x + 2, y, z) for x, y, z in shapes),
        tuple(vmem(2, 2, x, 1, z) for x, y, z in shapes),
        tuple(vmem(2, 2, x, 1, z) for x, y, z in shapes),
        tuple(vmem(7, x, y, z) for x, y, z in shapes[:3]),
        tuple(vmem(x, y, z) for x, y, z in shapes[:3]),
        vmem(2, 2, ny, wide),
        vmem(2, 2, nx, 1, wide),
        vmem(2, 2, nx, 1, wide),
        vmem(2, nx, ny, LANES),
        vmem(2, nx, ny, LANES),
        vmem(2, groups, ny, LANES),
        vmem(2, groups, ny, LANES),
        dma((4, 4, 2)), dma((4, 4, 2)), dma((4,)), dma((4,)), dma((4,)), dma((4,)),
    ]
    spec = pl.BlockSpec(memory_space=pltpu.VMEM)
    return pl.pallas_call(
        functools.partial(kernel, (nx, ny, nz), names),
        out_shape=jax.ShapeDtypeStruct(right_side.shape, f32),
        in_specs=[spec] * 3,
        out_specs=spec,
        scratch_shapes=scratch,
        compiler_params=pltpu.CompilerParams(
            collective_id=0, has_side_effects=True, vmem_limit_bytes=60 * 1024 * 1024),
    )(right_side, coefficients, first_guess)


def solution(mesh):
    names = tuple(mesh.axis_names)
    in_specs = (P(*names), P(None, *names), P(*names))
    return jax.shard_map(
        functools.partial(body, names), mesh=mesh, in_specs=in_specs, out_specs=P(*names),
        check_vma=False)
```

profile of v0, /device:TPU:0, one launch (start us, length us, event | category | flops | bytes accessed | tf_op | source)
XLA Modules:
  0.0 73.7 jit_solution(9022506723661265912)
XLA Ops:
  0.0 72.0 %shard_map.37 = f32[16,16,256]{2,1,0:T(8,128)} custom-call(f32[16,16,256]{2,1,0:T(8,128)} %b_ref.1, f32[4,16,16,256]{3,2,1,0:T(8,128)} %k_ref.1, f32[16,16,256]{2,1,0:T(8,128)} %g_ref.1), custom_call_target="tpu_custom_call" | custom-call | tf_op jit(solution)/shard_map/pallas_call | solution.py:443
  72.0 1.7 %copy.5 = f32[16,16,256]{2,1,0:T(8,128)} copy(f32[16,16,256]{2,1,0:T(8,128)} %shard_map.37) | data formatting | bytes 524288
where the time goes:
time: 73.9 us; the launch traced here: 73.7 us
  Pallas kernels  72 us (97%)
  local copies, waits for them, and re-layouts  1.67 us (2%)
    pallas_call x1, Pallas kernels, body(): pl.pallas_call(functools.partial(kernel, (nx, ny, nz), names), out_shape=...  72 us
    unnamed x1, local copies, waits for them, and re-layouts  1.67 us

commit v1 on v0

--- a/solution.py
+++ b/solution.py
@@ -451,9 +451,468 @@
     )(right_side, coefficients, first_guess)
 
 
+def slab_kernel(sizes, mesh_counts, names, b_hbm, k_hbm, g_hbm, out_ref, *scratch):
+    (stage, sb, rb, field, ub, bb, rr, fw, cells, ms, fs, es, tmp, so, ro,
+     in_sem, send, recv, zsend, zrecv, gsend, grecv, osend, orecv) = scratch
+    nx, ny, nz = sizes
+    cx, cy, cz = mesh_counts
+    group = cx * cy
+    slab = nz // group
+    pieces = LANES // slab
+    rows_of = nx // pieces
+    deep = 2 * SWEEPS
+    near = SWEEPS
+    span = LANES // cx
+    gx, gy, gz = (lax.axis_index(n) for n in names)
+    me = gx * cy + gy
+
+    def slab_of(x, y, z):
+        p = x * cy + y + lax.rem(x, 2) * (cy - 1 - 2 * y)
+        return p + lax.rem(z, 2) * (group - 1 - 2 * p)
+
+    def device_of(s, z):
+        p = s + lax.rem(z, 2) * (group - 1 - 2 * s)
+        x, t = p // cy, lax.rem(p, cy)
+        return x, t + lax.rem(x, 2) * (cy - 1 - 2 * t)
+
+    mine = slab_of(gx, gy, gz)
+    chain = gz * group + mine
+    has_prev, has_next = chain > 0, chain < cz * group - 1
+
+    def neighbour(step):
+        c = chain + step
+        c = jnp.clip(c, 0, cz * group - 1)
+        z, s = c // group, lax.rem(c, group)
+        x, y = device_of(s, z)
+        return {names[0]: x, names[1]: y, names[2]: z}
+
+    prev_id, next_id = neighbour(-1), neighbour(1)
+    across_prev = has_prev & (mine == 0)
+    across_next = has_next & (mine == group - 1)
+
+    loads = [pltpu.make_async_copy(k_hbm.at[j], stage.at[j], in_sem.at[j]) for j in range(4)]
+    loads.append(pltpu.make_async_copy(g_hbm, stage.at[4], in_sem.at[4]))
+    loads.append(pltpu.make_async_copy(b_hbm, stage.at[5], in_sem.at[5]))
+    for c in loads:
+        c.start()
+
+    def peer(rel):
+        return lax.rem(gx + rel // cy, cx), lax.rem(gy + rel % cy, cy)
+
+    barrier = pltpu.get_barrier_semaphore()
+    for rel in range(1, group):
+        x, y = peer(rel)
+        pl.semaphore_signal(barrier, inc=1, device_id={names[0]: x, names[1]: y}, device_id_type=MESH)
+
+    @pl.when(across_prev)
+    def _():
+        pl.semaphore_signal(barrier, inc=1, device_id=prev_id, device_id_type=MESH)
+
+    @pl.when(across_next)
+    def _():
+        pl.semaphore_signal(barrier, inc=1, device_id=next_id, device_id_type=MESH)
+
+    @pl.when(jnp.logical_not(has_prev))
+    def _():
+        field[:, :, 0:deep] = jnp.zeros((4, nx, deep, LANES), jnp.float32)
+        ub[:, 0:near] = jnp.zeros((nx, near, LANES), jnp.float32)
+        for g in range(3):
+            x = fs[g].shape[1]
+            fs[g][:, :, 0:near] = jnp.zeros((CYCLES, x, near, LANES), jnp.float32)
+
+    @pl.when(jnp.logical_not(has_next))
+    def _():
+        field[:, :, slab + deep:] = jnp.zeros((4, nx, deep, LANES), jnp.float32)
+        ub[:, slab + near:] = jnp.zeros((nx, near, LANES), jnp.float32)
+        for g in range(3):
+            x, rows = fs[g].shape[1:3]
+            fs[g][:, :, rows - near:] = jnp.zeros((CYCLES, x, near, LANES), jnp.float32)
+
+    def lane_of(shape):
+        return iota(shape, len(shape) - 1)
+
+    tile_lane = lane_of((ny, LANES))
+
+    def regroup(values):
+        values = list(values)
+        step = pieces // 2
+        while step:
+            width = slab * step
+            low = lax.rem(tile_lane // width, 2) == 0
+            for i in range(pieces):
+                if i & step == 0:
+                    a, c = values[i], values[i + step]
+                    values[i] = jnp.where(low, a, pltpu.roll(c, width, 1))
+                    values[i + step] = jnp.where(low, pltpu.roll(a, LANES - width, 1), c)
+            step //= 2
+        return values
+
+    def pack(f):
+        for xi in range(rows_of):
+            for t in range(nz // LANES):
+                parts = regroup(
+                    [stage[f, q * rows_of + xi, :, LANES * t:LANES * (t + 1)] for q in range(pieces)])
+                for q in range(pieces):
+                    sb[f, t * pieces + q, xi] = parts[q]
+
+    def spread_copies(f):
+        copies = []
+        for rel in range(1, group):
+            x, y = peer(rel)
+            copies.append(pltpu.make_async_remote_copy(
+                src_ref=sb.at[f, slab_of(x, y, gz)], dst_ref=rb.at[f, :, me],
+                send_sem=send.at[f, rel], recv_sem=recv.at[f, rel],
+                device_id={names[0]: x, names[1]: y}, device_id_type=MESH))
+        return copies
+
+    def z_copies(ref, own_low, own, halo, ssem, rsem):
+        up = pltpu.make_async_remote_copy(
+            src_ref=ref.at[:, pl.ds(own_low + own - halo, halo)], dst_ref=ref.at[:, pl.ds(own_low - halo, halo)],
+            send_sem=ssem.at[0], recv_sem=rsem.at[0], device_id=next_id, device_id_type=MESH)
+        down = pltpu.make_async_remote_copy(
+            src_ref=ref.at[:, pl.ds(own_low, halo)], dst_ref=ref.at[:, pl.ds(own_low + own, halo)],
+            send_sem=ssem.at[1], recv_sem=rsem.at[1], device_id=prev_id, device_id_type=MESH)
+        return up, down
+
+    def z_start(copies):
+        up, down = copies
+
+        @pl.when(has_next)
+        def _():
+            up.start()
+
+        @pl.when(has_prev)
+        def _():
+            down.start()
+
+    def z_finish(copies):
+        up, down = copies
+
+        @pl.when(has_prev)
+        def _():
+            up.wait_recv()
+
+        @pl.when(has_next)
+        def _():
+            down.wait_recv()
+
+        @pl.when(has_next)
+        def _():
+            up.wait_send()
+
+        @pl.when(has_prev)
+        def _():
+            down.wait_send()
+
+    every = []
+    for f in range(6):
+        loads[f].wait()
+        pack(f)
+        if f == 0:
+            pl.semaphore_wait(
+                barrier, group - 1 + jnp.where(across_prev, 1, 0) + jnp.where(across_next, 1, 0))
+        copies = spread_copies(f)
+        for c in copies:
+            c.start()
+        every.append(copies)
+        rb[f, :, me] = sb[f, mine]
+
+    def arrive(f):
+        for c in every[f]:
+            c.wait_recv()
+        for xi in range(rows_of):
+            turned = rb[f, xi].reshape((LANES, LANES)).T
+            for q in range(pieces):
+                part = turned[q * slab:(q + 1) * slab]
+                x = q * rows_of + xi
+                if f < 4:
+                    field[f, x, deep:deep + slab] = part
+                elif f == 4:
+                    ub[x, near:near + slab] = part
+                else:
+                    bb[x] = part
+
+    halos = []
+    for f in range(5):
+        arrive(f)
+        if f < 4:
+            halos.append(z_copies(field.at[f], deep, slab, deep, zsend.at[f], zrecv.at[f]))
+        else:
+            halos.append(z_copies(ub, near, slab, near, zsend.at[f], zrecv.at[f]))
+        z_start(halos[-1])
+
+    wide_rows = slab + 2 * near
+    first_row, last_row = deep - near, deep + slab + near
+    half = span // 2
+    r, c = iota((2 * LANES, LANES), 0), iota((2 * LANES, LANES), 1)
+    lane = lax.rem(r, LANES)
+    y_mean = jnp.where(
+        (r // LANES == lax.rem(c, span) // half) & (lane // span == c // span)
+        & (lax.rem(lane, span) // 2 == lax.rem(c, half)), 0.5, 0.0).astype(jnp.bfloat16)
+    r, c = iota((LANES, 2 * LANES), 0), iota((LANES, 2 * LANES), 1)
+    lane = lax.rem(c, LANES)
+    here = (c // LANES == lax.rem(r, span) // half) & (lane // span == r // span)
+    fine_y = lax.rem(lane, span)
+    main = fine_y // 2
+    side = jnp.where(lax.rem(fine_y, 2) == 1, main + 1, main - 1)
+    coarse_y = lax.rem(r, half)
+    y_spread = jnp.where(
+        here & (coarse_y == main), 0.75, jnp.where(here & (coarse_y == side), 0.25, 0.0)).astype(jnp.bfloat16)
+    folds = nx // 2
+
+    def fold_y(rows_low, rows_high):
+        n = rows_low.shape[0] * rows_low.shape[1]
+        both = jnp.concatenate([rows_low.reshape((n, LANES)), rows_high.reshape((n, LANES))], 1)
+        return spread(both, y_mean).reshape(rows_low.shape)
+
+    for f in range(4):
+        z_finish(halos[f])
+        factors = [0.25 if f == d else 1.0 for d in range(3)]
+        for i in range(nx // 2):
+            cells[0][f, i] = (0.5 * factors[0]) * (
+                field[f, 2 * i, first_row:last_row] + field[f, 2 * i + 1, first_row:last_row])
+        cells[1][f] = fold_y(
+            field[f, 0:folds, first_row:last_row], field[f, folds:nx, first_row:last_row]) * factors[1]
+        coarse_rows = slab // 2 + 2 * near
+        for x in range(nx):
+            cells[2][f, x] = (0.5 * factors[2]) * (
+                field[f, x, pl.ds(0, coarse_rows, stride=2)] + field[f, x, pl.ds(1, coarse_rows, stride=2)])
+
+    def masks(shape, width):
+        lanes = lane_of(shape)
+        y = lax.rem(lanes, width)
+        return y != 0, y != width - 1, lanes >= width, lanes < LANES - width
+
+    def x_pair(get, i, count, width):
+        below = get(i - 1) if i > 0 else pltpu.roll(get(count - 1), width, 1)
+        above = get(i + 1) if i < count - 1 else pltpu.roll(get(0), LANES - width, 1)
+        return below, above
+
+    def weights(k, i, count, width, z_pair):
+        y_low, y_high, x_low, x_high = masks(k(3, i).shape, width)
+        k0, k1, k2 = k(0, i), k(1, i), k(2, i)
+        below, above = x_pair(lambda p: k(0, p), i, count, width)
+        if i == 0:
+            below = jnp.where(x_low, below, 0.0)
+        if i == count - 1:
+            above = jnp.where(x_high, above, 0.0)
+        around = [
+            (k0, below, x_low if i == 0 else None), (k0, above, x_high if i == count - 1 else None),
+            (k1, jnp.where(y_low, pltpu.roll(k1, 1, 1), 0.0), y_low),
+            (k1, jnp.where(y_high, pltpu.roll(k1, LANES - 1, 1), 0.0), y_high),
+        ]
+        around += [(k2, other, None) for other in z_pair]
+        total = k(3, i)
+        found = []
+        for middle, other, keep in around:
+            w = 0.5 * (middle + other)
+            total = total + w
+            found.append(w if keep is None else jnp.where(keep, w, 0.0))
+        return found, total
+
+    widths = (span, half, span)
+    for g in range(3):
+        count, rows = cells[g].shape[1:3]
+        for i in range(count):
+            k2 = cells[g][2, i]
+            z_pair = (pltpu.roll(k2, 1, 0), pltpu.roll(k2, rows - 1, 0))
+            w, total = weights(lambda j, p: cells[g][j, p], i, count, widths[g], z_pair)
+            inside = cells[g][3, i] > 0.0
+            scale = jnp.where(inside, relaxation / jnp.where(inside, total, 1.0), 0.0)
+            ms[g][6, i] = scale
+            for j in range(6):
+                ms[g][j, i] = w[j] * scale
+    own = slice(deep, deep + slab)
+    for i in range(nx):
+        z_pair = (field[2, i, deep - 1:deep + slab - 1], field[2, i, deep + 1:deep + slab + 1])
+        w, total = weights(lambda j, p: field[j, p, own], i, nx, span, z_pair)
+        for j in range(6):
+            fw[j, i] = w[j]
+        fw[6, i] = total
+
+    z_finish(halos[4])
+    arrive(5)
+
+    def sweep(g, src, dst):
+        count, rows = src.shape[0:2]
+        m, f = ms[g], fs[g]
+        for i in range(count):
+            middle = src[i]
+            below, above = x_pair(lambda p: src[p], i, count, widths[g])
+            new = (1.0 - relaxation) * middle + f[cycle, i]
+            new = new + m[0, i] * below
+            new = new + m[1, i] * above
+            new = new + m[2, i] * pltpu.roll(middle, 1, 1)
+            new = new + m[3, i] * pltpu.roll(middle, LANES - 1, 1)
+            new = new + m[4, i] * pltpu.roll(middle, 1, 0)
+            new = new + m[5, i] * pltpu.roll(middle, rows - 1, 0)
+            dst[i] = new
+
+    for cycle in range(CYCLES):
+        for i in range(nx):
+            u = ub[i, near:near + slab]
+            below, above = x_pair(lambda p: ub[p, near:near + slab], i, nx, span)
+            residual = bb[i] - fw[6, i] * u
+            residual = residual + fw[0, i] * below
+            residual = residual + fw[1, i] * above
+            residual = residual + fw[2, i] * pltpu.roll(u, 1, 1)
+            residual = residual + fw[3, i] * pltpu.roll(u, LANES - 1, 1)
+            residual = residual + fw[4, i] * ub[i, near - 1:near + slab - 1]
+            residual = residual + fw[5, i] * ub[i, near + 1:near + slab + 1]
+            rr[i] = residual
+        for x in range(nx):
+            first = 0.5 * (rr[x, pl.ds(0, slab // 2, stride=2)] + rr[x, pl.ds(1, slab // 2, stride=2)])
+            fs[2][cycle, x, near:near + slab // 2] = ms[2][6, x, near:near + slab // 2] * first
+        for i in range(nx // 2):
+            first = 0.5 * (rr[2 * i] + rr[2 * i + 1])
+            fs[0][cycle, i, near:near + slab] = ms[0][6, i, near:near + slab] * first
+        first = fold_y(rr[0:folds], rr[folds:nx])
+        fs[1][cycle, :, near:near + slab] = ms[1][6, :, near:near + slab] * first
+        moves = []
+        for g in range(3):
+            rows = fs[g].shape[2]
+            moves.append(z_copies(
+                fs[g].at[cycle], near, rows - 2 * near, near, gsend.at[cycle, g], grecv.at[cycle, g]))
+            z_start(moves[-1])
+        for g in range(3):
+            z_finish(moves[g])
+            sweep(g, fs[g].at[cycle], es[g].at[0])
+
+        @pl.loop(0, SWEEPS - 2)
+        def _(repeat):
+            old = lax.rem(repeat, 2)
+            for g in range(3):
+                sweep(g, es[g].at[old], es[g].at[1 - old])
+
+        last = (SWEEPS - 2) % 2
+        keep = wide_rows if cycle < CYCLES - 1 else slab
+        low = 0 if cycle < CYCLES - 1 else near
+        taken = slice(low, low + keep)
+        lanes = lane_of((keep, LANES))
+        e = es[1][last, :, taken].reshape((folds * keep, LANES))
+        from_y = spread(e, y_spread)
+        coarse_low = near - (near - low) // 2
+        count = keep // 2
+        for x in range(nx):
+            middle = es[2][last, x, coarse_low:coarse_low + count]
+            lower = es[2][last, x, coarse_low - 1:coarse_low + count - 1]
+            upper = es[2][last, x, coarse_low + 1:coarse_low + count + 1]
+            tmp[x, pl.ds(0, count, stride=2)] = 0.75 * middle + 0.25 * lower
+            tmp[x, pl.ds(1, count, stride=2)] = 0.75 * middle + 0.25 * upper
+        for i in range(nx // 2):
+            middle = es[0][last, i, taken]
+            below, above = x_pair(lambda p: es[0][last, p, taken], i, nx // 2, span)
+            if i == 0:
+                below = jnp.where(lanes >= span, below, 0.0)
+            if i == nx // 2 - 1:
+                above = jnp.where(lanes < LANES - span, above, 0.0)
+            for odd, other in ((0, below), (1, above)):
+                x = 2 * i + odd
+                from_x = 0.75 * middle + 0.25 * other
+                fold, xi = x // folds, x % folds
+                mid_y = from_y[xi * keep:(xi + 1) * keep, LANES * fold:LANES * (fold + 1)]
+                update = (from_x + mid_y) + tmp[x, 0:keep]
+                ub[x, taken] = ub[x, taken] + blending * update
+        if cycle < CYCLES - 1:
+            @pl.when(jnp.logical_not(has_prev))
+            def _():
+                ub[:, 0:near] = jnp.zeros((nx, near, LANES), jnp.float32)
+
+            @pl.when(jnp.logical_not(has_next))
+            def _():
+                ub[:, slab + near:] = jnp.zeros((nx, near, LANES), jnp.float32)
+
+    backs = []
+    for xi in range(rows_of):
+        block = jnp.concatenate([ub[q * rows_of + xi, near:near + slab] for q in range(pieces)], 0)
+        turned = block.T
+        for j in range(group):
+            so[j, xi] = turned[j * ny:(j + 1) * ny]
+    for rel in range(1, group):
+        x, y = peer(rel)
+        backs.append(pltpu.make_async_remote_copy(
+            src_ref=so.at[x * cy + y], dst_ref=ro.at[mine], send_sem=osend.at[rel], recv_sem=orecv.at[rel],
+            device_id={names[0]: x, names[1]: y}, device_id_type=MESH))
+    for c in backs:
+        c.start()
+    ro[mine] = so[me]
+    for c in backs:
+        c.wait_recv()
+    for xi in range(rows_of):
+        for t in range(nz // LANES):
+            parts = regroup([ro[t * pieces + q, xi] for q in range(pieces)])
+            for q in range(pieces):
+                out_ref[q * rows_of + xi, :, LANES * t:LANES * (t + 1)] = parts[q]
+    for copies in every + [backs]:
+        for c in copies:
+            c.wait_send()
+
+
+def slab_fits(shape, counts):
+    nx, ny, nz = shape
+    cx, cy, _ = counts
+    group = cx * cy
+    if nz % group or ny * group != LANES or LANES % (2 * cx):
+        return False
+    slab = nz // group
+    pieces = LANES // slab
+    return (
+        slab * pieces == LANES and pieces & (pieces - 1) == 0 and nx % (2 * pieces) == 0
+        and slab % 16 == 0 and slab >= 2 * SWEEPS and nz % LANES == 0)
+
+
+def slab_body(names, counts, right_side, coefficients, first_guess):
+    nx, ny, nz = right_side.shape
+    f32 = jnp.float32
+    vmem = lambda *shape: pltpu.VMEM(shape, f32)
+    dma = pltpu.SemaphoreType.DMA
+    group = counts[0] * counts[1]
+    slab = nz // group
+    rows_of = nx // (LANES // slab)
+    near, deep = SWEEPS, 2 * SWEEPS
+    wide = slab + 2 * near
+    shapes = ((nx // 2, wide), (nx // 2, wide), (nx, slab // 2 + 2 * near))
+    blocks = (group, rows_of, ny, LANES)
+    scratch = [
+        vmem(6, nx, ny, nz),
+        vmem(6, *blocks),
+        vmem(6, rows_of, group, ny, LANES),
+        vmem(4, nx, slab + 2 * deep, LANES),
+        vmem(nx, wide, LANES),
+        vmem(nx, slab, LANES),
+        vmem(nx, slab, LANES),
+        vmem(7, nx, slab, LANES),
+        tuple(vmem(4, x, z, LANES) for x, z in shapes),
+        tuple(vmem(7, x, z, LANES) for x, z in shapes),
+        tuple(vmem(CYCLES, x, z, LANES) for x, z in shapes),
+        tuple(vmem(2, x, z, LANES) for x, z in shapes),
+        vmem(nx, wide, LANES),
+        vmem(*blocks),
+        vmem(*blocks),
+        dma((6,)), dma((6, group)), dma((6, group)), dma((5, 2)), dma((5, 2)),
+        dma((CYCLES, 3, 2)), dma((CYCLES, 3, 2)), dma((group,)), dma((group,)),
+    ]
+    hbm = pl.BlockSpec(memory_space=pl.ANY)
+    return pl.pallas_call(
+        functools.partial(slab_kernel, (nx, ny, nz), counts, names),
+        out_shape=jax.ShapeDtypeStruct(right_side.shape, f32),
+        in_specs=[hbm] * 3,
+        out_specs=pl.BlockSpec(memory_space=pltpu.VMEM),
+        scratch_shapes=scratch,
+        compiler_params=pltpu.CompilerParams(
+            collective_id=0, has_side_effects=True, vmem_limit_bytes=60 * 1024 * 1024),
+    )(right_side, coefficients, first_guess)
+
+
 def solution(mesh):
     names = tuple(mesh.axis_names)
+    counts = tuple(mesh.shape[n] for n in names)
     in_specs = (P(*names), P(None, *names), P(*names))
+
+    def local(right_side, coefficients, first_guess):
+        if slab_fits(right_side.shape, counts):
+            return slab_body(names, counts, right_side, coefficients, first_guess)
+        return body(names, right_side, coefficients, first_guess)
+
     return jax.shard_map(
-        functools.partial(body, names), mesh=mesh, in_specs=in_specs, out_specs=P(*names),
-        check_vma=False)
+        local, mesh=mesh, in_specs=in_specs, out_specs=P(*names), check_vma=False)

time: 73.9 us -> 54.9 us (0.74)
  Pallas kernels: 72 us -> 53 us
    pallas_call x1, Pallas kernels: 72 us -> 53 us  [slab_body(): pl.pallas_call(functools.partial(slab_kernel, (nx, ny, nz), counts, names...]
where the time goes in v1:
time: 54.9 us; the launch traced here: 54.7 us
  Pallas kernels  53 us (97%)
  local copies, waits for them, and re-layouts  1.67 us (3%)
    pallas_call x1, Pallas kernels, slab_body(): pl.pallas_call(functools.partial(slab_kernel, (nx, ny, nz), counts, names...  53 us
    unnamed x1, local copies, waits for them, and re-layouts  1.67 us

profile of v1, /device:TPU:0, one launch (start us, length us, event | category | flops | bytes accessed | tf_op | source)
XLA Modules:
  0.0 54.7 jit_solution(12533798052854497357)
XLA Ops:
  0.0 53.0 %shard_map.37 = f32[16,16,256]{2,1,0:T(8,128)} custom-call(f32[16,16,256]{2,1,0:T(8,128)} %b_hbm.1, f32[4,16,16,256]{3,2,1,0:T(8,128)} %k_hbm.1, f32[16,16,256]{2,1,0:T(8,128)} %g_hbm.1), custom_call_target="tpu_custom_call" | custom-call | tf_op jit(solution)/shard_map/pallas_call | solution.py:896
  53.0 1.7 %copy.5 = f32[16,16,256]{2,1,0:T(8,128)} copy(f32[16,16,256]{2,1,0:T(8,128)} %shard_map.37) | data formatting | bytes 524288

commit v2 on v1

--- a/solution.py
+++ b/solution.py
@@ -452,16 +452,16 @@
 
 
 def slab_kernel(sizes, mesh_counts, names, b_hbm, k_hbm, g_hbm, out_ref, *scratch):
-    (stage, sb, rb, field, ub, bb, rr, fw, cells, ms, fs, es, tmp, so, ro,
-     in_sem, send, recv, zsend, zrecv, gsend, grecv, osend, orecv) = scratch
+    (stage, sb, rb, field, ub, bb, rr, fw, cells, ms, fs, es, tmp, so, ro, hx, hys, hyr, hzs, hz, ex,
+     in_sem, send, recv, zsend, zrecv, gsend, grecv, osend, orecv, hsend, hrecv, esend, erecv) = scratch
     nx, ny, nz = sizes
     cx, cy, cz = mesh_counts
     group = cx * cy
     slab = nz // group
     pieces = LANES // slab
     rows_of = nx // pieces
-    deep = 2 * SWEEPS
     near = SWEEPS
+    nears = (near, near, near // 2)
     span = LANES // cx
     gx, gy, gz = (lax.axis_index(n) for n in names)
     me = gx * cy + gy
@@ -487,8 +487,9 @@
         return {names[0]: x, names[1]: y, names[2]: z}
 
     prev_id, next_id = neighbour(-1), neighbour(1)
-    across_prev = has_prev & (mine == 0)
-    across_next = has_next & (mine == group - 1)
+    place, counts = (gx, gy, gz), (cx, cy, cz)
+    has_low = [q > 0 for q in place]
+    has_high = [q < c - 1 for q, c in zip(place, counts)]
 
     loads = [pltpu.make_async_copy(k_hbm.at[j], stage.at[j], in_sem.at[j]) for j in range(4)]
     loads.append(pltpu.make_async_copy(g_hbm, stage.at[4], in_sem.at[4]))
@@ -504,29 +505,29 @@
         x, y = peer(rel)
         pl.semaphore_signal(barrier, inc=1, device_id={names[0]: x, names[1]: y}, device_id_type=MESH)
 
-    @pl.when(across_prev)
+    @pl.when(has_low[2])
     def _():
-        pl.semaphore_signal(barrier, inc=1, device_id=prev_id, device_id_type=MESH)
-
-    @pl.when(across_next)
+        pl.semaphore_signal(barrier, inc=1, device_id={names[2]: gz - 1}, device_id_type=MESH)
+
+    @pl.when(has_high[2])
     def _():
-        pl.semaphore_signal(barrier, inc=1, device_id=next_id, device_id_type=MESH)
+        pl.semaphore_signal(barrier, inc=1, device_id={names[2]: gz + 1}, device_id_type=MESH)
 
     @pl.when(jnp.logical_not(has_prev))
     def _():
-        field[:, :, 0:deep] = jnp.zeros((4, nx, deep, LANES), jnp.float32)
-        ub[:, 0:near] = jnp.zeros((nx, near, LANES), jnp.float32)
+        field[:, :, 0:near] = jnp.zeros((4, nx, near, LANES), jnp.float32)
         for g in range(3):
             x = fs[g].shape[1]
-            fs[g][:, :, 0:near] = jnp.zeros((CYCLES, x, near, LANES), jnp.float32)
+            fs[g][:, :, 0:nears[g]] = jnp.zeros((CYCLES, x, nears[g], LANES), jnp.float32)
+        ex[:, :, 0:nears[2]] = jnp.zeros((CYCLES, nx, nears[2], LANES), jnp.float32)
 
     @pl.when(jnp.logical_not(has_next))
     def _():
-        field[:, :, slab + deep:] = jnp.zeros((4, nx, deep, LANES), jnp.float32)
-        ub[:, slab + near:] = jnp.zeros((nx, near, LANES), jnp.float32)
+        field[:, :, slab + near:] = jnp.zeros((4, nx, near, LANES), jnp.float32)
         for g in range(3):
             x, rows = fs[g].shape[1:3]
-            fs[g][:, :, rows - near:] = jnp.zeros((CYCLES, x, near, LANES), jnp.float32)
+            fs[g][:, :, rows - nears[g]:] = jnp.zeros((CYCLES, x, nears[g], LANES), jnp.float32)
+        ex[:, :, slab // 2 + nears[2]:] = jnp.zeros((CYCLES, nx, nears[2], LANES), jnp.float32)
 
     def lane_of(shape):
         return iota(shape, len(shape) - 1)
@@ -551,7 +552,7 @@
         for xi in range(rows_of):
             for t in range(nz // LANES):
                 parts = regroup(
-                    [stage[f, q * rows_of + xi, :, LANES * t:LANES * (t + 1)] for q in range(pieces)])
+                    [stage[5 if f == 4 else f, q * rows_of + xi, :, LANES * t:LANES * (t + 1)] for q in range(pieces)])
                 for q in range(pieces):
                     sb[f, t * pieces + q, xi] = parts[q]
 
@@ -604,18 +605,115 @@
         def _():
             down.wait_send()
 
+    for side in range(2):
+        absent = [jnp.logical_not((has_low, has_high)[side][axis]) for axis in range(3)]
+
+        @pl.when(absent[0])
+        def _():
+            hx[:, side] = jnp.zeros((2, ny, nz), jnp.float32)
+
+        @pl.when(absent[1])
+        def _():
+            hyr[:, side] = jnp.zeros((2, nx, 1, nz), jnp.float32)
+
+        @pl.when(absent[2])
+        def _():
+            hz[side] = jnp.zeros((ny, LANES), jnp.float32)
+
+    faces = []
+    for a in range(2):
+        for axis in range(3 if a == 0 else 2):
+            v = 4 if a == 0 else axis
+            for side in range(2):
+                src = (stage.at[v, (0, nx - 1)[side]], hys.at[a, side], hzs.at[side])[axis]
+                dst = (hx.at[a, 1 - side], hyr.at[a, 1 - side], hz.at[1 - side])[axis]
+                faces.append((
+                    pltpu.make_async_remote_copy(
+                        src_ref=src, dst_ref=dst, send_sem=hsend.at[a, axis, side], recv_sem=hrecv.at[a, axis, side],
+                        device_id={names[axis]: place[axis] + (-1, 1)[side]}, device_id_type=MESH),
+                    (has_low, has_high)[side][axis], (has_high, has_low)[side][axis]))
+
+    for f in (4, 0, 1, 2):
+        loads[f].wait()
+    for a in range(2):
+        for side in range(2):
+            row = (0, ny - 1)[side]
+            hys[a, side] = stage[4 if a == 0 else 1, :, row:row + 1, :]
+    for side in range(2):
+        edge = jnp.zeros((ny, LANES), jnp.float32)
+        for a in range(2):
+            for i in range(nx):
+                v, to = 4 if a == 0 else 2, a * nx + i
+                if side == 0:
+                    rolled = pltpu.roll(stage[v, i, :, 0:LANES], to, 1) if to else stage[v, i, :, 0:LANES]
+                else:
+                    rolled = pltpu.roll(stage[v, i, :, nz - LANES:nz], to + 1, 1)
+                edge = jnp.where(tile_lane == to, rolled, edge)
+        hzs[side] = edge
+    pl.semaphore_wait(barrier, group - 1 + jnp.where(has_low[2], 1, 0) + jnp.where(has_high[2], 1, 0))
+    for c, goes, _ in faces:
+        @pl.when(goes)
+        def _():
+            c.start()
+
     every = []
-    for f in range(6):
-        loads[f].wait()
+
+    def send_out(f):
         pack(f)
-        if f == 0:
-            pl.semaphore_wait(
-                barrier, group - 1 + jnp.where(across_prev, 1, 0) + jnp.where(across_next, 1, 0))
         copies = spread_copies(f)
         for c in copies:
             c.start()
         every.append(copies)
         rb[f, :, me] = sb[f, mine]
+
+    for f in range(4):
+        if f == 3:
+            loads[3].wait()
+        send_out(f)
+    loads[5].wait()
+    for c, goes, comes in faces:
+        @pl.when(comes)
+        def _():
+            c.wait_recv()
+
+    tile_row = iota((ny, LANES), 0)
+    count_t = nz // LANES
+
+    def home_shifts(f, a, i, axis):
+        tiles_of = [stage[f, i, :, LANES * t:LANES * (t + 1)] for t in range(count_t)]
+        if axis == 0:
+            low = stage[f, i - 1] if i > 0 else hx[a, 0]
+            high = stage[f, i + 1] if i < nx - 1 else hx[a, 1]
+            cut = lambda v: [v[:, LANES * t:LANES * (t + 1)] for t in range(count_t)]
+            return list(zip(cut(low), cut(high)))
+        if axis == 1:
+            found = []
+            for t in range(count_t):
+                at = slice(LANES * t, LANES * (t + 1))
+                found.append((
+                    jnp.where(tile_row == 0, hyr[a, 0, i, :, at], pltpu.roll(tiles_of[t], 1, 0)),
+                    jnp.where(tile_row == ny - 1, hyr[a, 1, i, :, at], pltpu.roll(tiles_of[t], ny - 1, 0))))
+            return found
+        to = a * nx + i
+        ups = [pltpu.roll(hz[0], LANES - to, 1) if to else hz[0]] + [pltpu.roll(v, 1, 1) for v in tiles_of]
+        downs = [pltpu.roll(v, LANES - 1, 1) for v in tiles_of] + [pltpu.roll(hz[1], LANES - 1 - to, 1)]
+        return [
+            (jnp.where(tile_lane == 0, ups[t], ups[t + 1]),
+             jnp.where(tile_lane == LANES - 1, downs[t + 1], downs[t])) for t in range(count_t)]
+
+    for i in range(nx):
+        around = [(home_shifts(4, 0, i, axis), home_shifts(axis, 1, i, axis)) for axis in range(3)]
+        for t in range(count_t):
+            at = slice(LANES * t, LANES * (t + 1))
+            total = stage[3, i, :, at]
+            pulled = stage[5, i, :, at]
+            for axis in range(3):
+                middle = stage[axis, i, :, at]
+                for side in range(2):
+                    w = 0.5 * (middle + around[axis][1][t][side])
+                    total = total + w
+                    pulled = pulled + w * around[axis][0][t][side]
+            stage[5, i, :, at] = pulled - total * stage[4, i, :, at]
 
     def arrive(f):
         for c in every[f]:
@@ -626,23 +724,18 @@
                 part = turned[q * slab:(q + 1) * slab]
                 x = q * rows_of + xi
                 if f < 4:
-                    field[f, x, deep:deep + slab] = part
-                elif f == 4:
-                    ub[x, near:near + slab] = part
+                    field[f, x, near:near + slab] = part
                 else:
                     bb[x] = part
 
+    send_out(4)
     halos = []
-    for f in range(5):
+    for f in range(4):
         arrive(f)
-        if f < 4:
-            halos.append(z_copies(field.at[f], deep, slab, deep, zsend.at[f], zrecv.at[f]))
-        else:
-            halos.append(z_copies(ub, near, slab, near, zsend.at[f], zrecv.at[f]))
+        halos.append(z_copies(field.at[f], near, slab, near, zsend.at[f], zrecv.at[f]))
         z_start(halos[-1])
 
     wide_rows = slab + 2 * near
-    first_row, last_row = deep - near, deep + slab + near
     half = span // 2
     r, c = iota((2 * LANES, LANES), 0), iota((2 * LANES, LANES), 1)
     lane = lax.rem(r, LANES)
@@ -670,10 +763,10 @@
         factors = [0.25 if f == d else 1.0 for d in range(3)]
         for i in range(nx // 2):
             cells[0][f, i] = (0.5 * factors[0]) * (
-                field[f, 2 * i, first_row:last_row] + field[f, 2 * i + 1, first_row:last_row])
+                field[f, 2 * i] + field[f, 2 * i + 1])
         cells[1][f] = fold_y(
-            field[f, 0:folds, first_row:last_row], field[f, folds:nx, first_row:last_row]) * factors[1]
-        coarse_rows = slab // 2 + 2 * near
+            field[f, 0:folds], field[f, folds:nx]) * factors[1]
+        coarse_rows = slab // 2 + 2 * nears[2]
         for x in range(nx):
             cells[2][f, x] = (0.5 * factors[2]) * (
                 field[f, x, pl.ds(0, coarse_rows, stride=2)] + field[f, x, pl.ds(1, coarse_rows, stride=2)])
@@ -722,34 +815,50 @@
             ms[g][6, i] = scale
             for j in range(6):
                 ms[g][j, i] = w[j] * scale
-    own = slice(deep, deep + slab)
+    own = slice(near, near + slab)
     for i in range(nx):
-        z_pair = (field[2, i, deep - 1:deep + slab - 1], field[2, i, deep + 1:deep + slab + 1])
+        z_pair = (field[2, i, near - 1:near + slab - 1], field[2, i, near + 1:near + slab + 1])
         w, total = weights(lambda j, p: field[j, p, own], i, nx, span, z_pair)
         for j in range(6):
             fw[j, i] = w[j]
         fw[6, i] = total
 
-    z_finish(halos[4])
-    arrive(5)
-
-    def sweep(g, src, dst):
-        count, rows = src.shape[0:2]
+    arrive(4)
+
+    pad = 8
+
+    def plane(src, i, rows, shift=0):
+        if len(src.shape) == 2:
+            at = pad + i * rows + shift
+            return src[at:at + rows]
+        return pltpu.roll(src[i], -shift % rows, 0) if shift else src[i]
+
+    for g in range(3):
+        rows = es[g].shape[1]
+        es[g][:, 0:pad] = jnp.zeros((2, pad, LANES), jnp.float32)
+        es[g][:, rows - pad:] = jnp.zeros((2, pad, LANES), jnp.float32)
+
+    def sweep(g, src, dst, inner=False):
+        count, rows = fs[g].shape[1:3]
         m, f = ms[g], fs[g]
         for i in range(count):
-            middle = src[i]
-            below, above = x_pair(lambda p: src[p], i, count, widths[g])
+            middle = plane(src, i, rows)
+            below, above = x_pair(lambda p: plane(src, p, rows), i, count, widths[g])
             new = (1.0 - relaxation) * middle + f[cycle, i]
             new = new + m[0, i] * below
             new = new + m[1, i] * above
             new = new + m[2, i] * pltpu.roll(middle, 1, 1)
             new = new + m[3, i] * pltpu.roll(middle, LANES - 1, 1)
-            new = new + m[4, i] * pltpu.roll(middle, 1, 0)
-            new = new + m[5, i] * pltpu.roll(middle, rows - 1, 0)
-            dst[i] = new
+            new = new + m[4, i] * plane(src, i, rows, -1)
+            new = new + m[5, i] * plane(src, i, rows, 1)
+            if inner:
+                dst[i, nears[g]:rows - nears[g]] = new[nears[g]:rows - nears[g]]
+            else:
+                dst[pad + i * rows:pad + (i + 1) * rows] = new
 
     for cycle in range(CYCLES):
-        for i in range(nx):
+        left = rr if cycle else bb
+        for i in range(nx if cycle else 0):
             u = ub[i, near:near + slab]
             below, above = x_pair(lambda p: ub[p, near:near + slab], i, nx, span)
             residual = bb[i] - fw[6, i] * u
@@ -760,48 +869,67 @@
             residual = residual + fw[4, i] * ub[i, near - 1:near + slab - 1]
             residual = residual + fw[5, i] * ub[i, near + 1:near + slab + 1]
             rr[i] = residual
+        moves = {}
+
+        def send_first(g):
+            rows = fs[g].shape[2]
+            moves[g] = z_copies(
+                fs[g].at[cycle], nears[g], rows - 2 * nears[g], nears[g], gsend.at[cycle, g], grecv.at[cycle, g])
+            z_start(moves[g])
+
+        low2, high2 = nears[2], nears[2] + slab // 2
         for x in range(nx):
-            first = 0.5 * (rr[x, pl.ds(0, slab // 2, stride=2)] + rr[x, pl.ds(1, slab // 2, stride=2)])
-            fs[2][cycle, x, near:near + slab // 2] = ms[2][6, x, near:near + slab // 2] * first
+            first = 0.5 * (left[x, pl.ds(0, slab // 2, stride=2)] + left[x, pl.ds(1, slab // 2, stride=2)])
+            fs[2][cycle, x, low2:high2] = ms[2][6, x, low2:high2] * first
+        send_first(2)
         for i in range(nx // 2):
-            first = 0.5 * (rr[2 * i] + rr[2 * i + 1])
+            first = 0.5 * (left[2 * i] + left[2 * i + 1])
             fs[0][cycle, i, near:near + slab] = ms[0][6, i, near:near + slab] * first
-        first = fold_y(rr[0:folds], rr[folds:nx])
+        send_first(0)
+        first = fold_y(left[0:folds], left[folds:nx])
         fs[1][cycle, :, near:near + slab] = ms[1][6, :, near:near + slab] * first
-        moves = []
-        for g in range(3):
-            rows = fs[g].shape[2]
-            moves.append(z_copies(
-                fs[g].at[cycle], near, rows - 2 * near, near, gsend.at[cycle, g], grecv.at[cycle, g]))
-            z_start(moves[-1])
-        for g in range(3):
+        send_first(1)
+
+        z_finish(moves[2])
+        src = fs[2].at[cycle]
+        for repeat in range(nears[2] - 1):
+            sweep(2, src, es[2].at[repeat % 2])
+            src = es[2].at[repeat % 2]
+        sweep(2, src, ex.at[cycle], True)
+        middle_move = z_copies(ex.at[cycle], low2, slab // 2, low2, esend.at[cycle], erecv.at[cycle])
+        z_start(middle_move)
+        for g in range(2):
             z_finish(moves[g])
             sweep(g, fs[g].at[cycle], es[g].at[0])
 
         @pl.loop(0, SWEEPS - 2)
         def _(repeat):
             old = lax.rem(repeat, 2)
-            for g in range(3):
+            for g in range(2):
                 sweep(g, es[g].at[old], es[g].at[1 - old])
 
         last = (SWEEPS - 2) % 2
+        z_finish(middle_move)
+        src = ex.at[cycle]
+        for repeat in range(SWEEPS - 1 - nears[2]):
+            slot = (last + SWEEPS - nears[2] - repeat) % 2
+            sweep(2, src, es[2].at[slot])
+            src = es[2].at[slot]
         keep = wide_rows if cycle < CYCLES - 1 else slab
         low = 0 if cycle < CYCLES - 1 else near
         taken = slice(low, low + keep)
         lanes = lane_of((keep, LANES))
-        e = es[1][last, :, taken].reshape((folds * keep, LANES))
+        e_of = [functools.partial(plane, es[g].at[last], rows=fs[g].shape[2]) for g in range(3)]
+        e = jnp.concatenate([e_of[1](i)[taken] for i in range(folds)], 0)
         from_y = spread(e, y_spread)
-        coarse_low = near - (near - low) // 2
         count = keep // 2
         for x in range(nx):
-            middle = es[2][last, x, coarse_low:coarse_low + count]
-            lower = es[2][last, x, coarse_low - 1:coarse_low + count - 1]
-            upper = es[2][last, x, coarse_low + 1:coarse_low + count + 1]
+            middle, lower, upper = (e_of[2](x, shift=step)[low // 2:low // 2 + count] for step in (0, -1, 1))
             tmp[x, pl.ds(0, count, stride=2)] = 0.75 * middle + 0.25 * lower
             tmp[x, pl.ds(1, count, stride=2)] = 0.75 * middle + 0.25 * upper
         for i in range(nx // 2):
-            middle = es[0][last, i, taken]
-            below, above = x_pair(lambda p: es[0][last, p, taken], i, nx // 2, span)
+            middle = e_of[0](i)[taken]
+            below, above = x_pair(lambda p: e_of[0](p)[taken], i, nx // 2, span)
             if i == 0:
                 below = jnp.where(lanes >= span, below, 0.0)
             if i == nx // 2 - 1:
@@ -812,7 +940,7 @@
                 fold, xi = x // folds, x % folds
                 mid_y = from_y[xi * keep:(xi + 1) * keep, LANES * fold:LANES * (fold + 1)]
                 update = (from_x + mid_y) + tmp[x, 0:keep]
-                ub[x, taken] = ub[x, taken] + blending * update
+                ub[x, taken] = ub[x, taken] + blending * update if cycle else blending * update
         if cycle < CYCLES - 1:
             @pl.when(jnp.logical_not(has_prev))
             def _():
@@ -842,9 +970,14 @@
         for t in range(nz // LANES):
             parts = regroup([ro[t * pieces + q, xi] for q in range(pieces)])
             for q in range(pieces):
-                out_ref[q * rows_of + xi, :, LANES * t:LANES * (t + 1)] = parts[q]
+                x, at = q * rows_of + xi, slice(LANES * t, LANES * (t + 1))
+                out_ref[x, :, at] = stage[4, x, :, at] + parts[q]
     for copies in every + [backs]:
         for c in copies:
+            c.wait_send()
+    for c, goes, _ in faces:
+        @pl.when(goes)
+        def _():
             c.wait_send()
 
 
@@ -858,7 +991,7 @@
     pieces = LANES // slab
     return (
         slab * pieces == LANES and pieces & (pieces - 1) == 0 and nx % (2 * pieces) == 0
-        and slab % 16 == 0 and slab >= 2 * SWEEPS and nz % LANES == 0)
+        and slab % 16 == 0 and slab >= 2 * SWEEPS and nz % LANES == 0 and 2 * nx <= LANES)
 
 
 def slab_body(names, counts, right_side, coefficients, first_guess):
@@ -869,15 +1002,15 @@
     group = counts[0] * counts[1]
     slab = nz // group
     rows_of = nx // (LANES // slab)
-    near, deep = SWEEPS, 2 * SWEEPS
+    near = SWEEPS
     wide = slab + 2 * near
-    shapes = ((nx // 2, wide), (nx // 2, wide), (nx, slab // 2 + 2 * near))
+    shapes = ((nx // 2, wide), (nx // 2, wide), (nx, slab // 2 + near))
     blocks = (group, rows_of, ny, LANES)
     scratch = [
         vmem(6, nx, ny, nz),
-        vmem(6, *blocks),
-        vmem(6, rows_of, group, ny, LANES),
-        vmem(4, nx, slab + 2 * deep, LANES),
+        vmem(5, *blocks),
+        vmem(5, rows_of, group, ny, LANES),
+        vmem(4, nx, wide, LANES),
         vmem(nx, wide, LANES),
         vmem(nx, slab, LANES),
         vmem(nx, slab, LANES),
@@ -885,12 +1018,15 @@
         tuple(vmem(4, x, z, LANES) for x, z in shapes),
         tuple(vmem(7, x, z, LANES) for x, z in shapes),
         tuple(vmem(CYCLES, x, z, LANES) for x, z in shapes),
-        tuple(vmem(2, x, z, LANES) for x, z in shapes),
+        tuple(vmem(2, x * z + 16, LANES) for x, z in shapes),
         vmem(nx, wide, LANES),
         vmem(*blocks),
         vmem(*blocks),
-        dma((6,)), dma((6, group)), dma((6, group)), dma((5, 2)), dma((5, 2)),
+        vmem(2, 2, ny, nz), vmem(2, 2, nx, 1, nz), vmem(2, 2, nx, 1, nz), vmem(2, ny, LANES),
+        vmem(2, ny, LANES), vmem(CYCLES, *shapes[2], LANES),
+        dma((6,)), dma((5, group)), dma((5, group)), dma((4, 2)), dma((4, 2)),
         dma((CYCLES, 3, 2)), dma((CYCLES, 3, 2)), dma((group,)), dma((group,)),
+        dma((2, 3, 2)), dma((2, 3, 2)), dma((CYCLES, 2)), dma((CYCLES, 2)),
     ]
     hbm = pl.BlockSpec(memory_space=pl.ANY)
     return pl.pallas_call(

time: 54.9 us -> 47.5 us (0.87)
  Pallas kernels: 53 us -> 45.7 us
    pallas_call x1, Pallas kernels: 53 us -> 45.7 us  [slab_body(): pl.pallas_call(functools.partial(slab_kernel, (nx, ny, nz), counts, names...]
where the time goes in v2:
time: 47.5 us; the launch traced here: 47.4 us
  Pallas kernels  45.7 us (96%)
  local copies, waits for them, and re-layouts  1.67 us (4%)
    pallas_call x1, Pallas kernels, slab_body(): pl.pallas_call(functools.partial(slab_kernel, (nx, ny, nz), counts, names...  45.7 us
    unnamed x1, local copies, waits for them, and re-layouts  1.67 us

profile of v2, /device:TPU:0, one launch (start us, length us, event | category | flops | bytes accessed | tf_op | source)
XLA Modules:
  0.0 47.4 jit_solution(18195277246134904084)
XLA Ops:
  0.0 45.7 %shard_map.37 = f32[16,16,256]{2,1,0:T(8,128)} custom-call(f32[16,16,256]{2,1,0:T(8,128)} %b_hbm.1, f32[4,16,16,256]{3,2,1,0:T(8,128)} %k_hbm.1, f32[16,16,256]{2,1,0:T(8,128)} %g_hbm.1), custom_call_target="tpu_custom_call" | custom-call | tf_op jit(solution)/shard_map/pallas_call | solution.py:1032
  45.7 1.7 %copy.5 = f32[16,16,256]{2,1,0:T(8,128)} copy(f32[16,16,256]{2,1,0:T(8,128)} %shard_map.37) | data formatting | bytes 524288

commit v3 on v2

--- a/solution.py
+++ b/solution.py
@@ -494,8 +494,9 @@
     loads = [pltpu.make_async_copy(k_hbm.at[j], stage.at[j], in_sem.at[j]) for j in range(4)]
     loads.append(pltpu.make_async_copy(g_hbm, stage.at[4], in_sem.at[4]))
     loads.append(pltpu.make_async_copy(b_hbm, stage.at[5], in_sem.at[5]))
-    for c in loads:
-        c.start()
+    order = (2, 0, 1, 3)
+    for f in order + (4, 5):
+        loads[f].start()
 
     def peer(rel):
         return lax.rem(gx + rel // cy, cx), lax.rem(gy + rel % cy, cy)
@@ -512,22 +513,6 @@
     @pl.when(has_high[2])
     def _():
         pl.semaphore_signal(barrier, inc=1, device_id={names[2]: gz + 1}, device_id_type=MESH)
-
-    @pl.when(jnp.logical_not(has_prev))
-    def _():
-        field[:, :, 0:near] = jnp.zeros((4, nx, near, LANES), jnp.float32)
-        for g in range(3):
-            x = fs[g].shape[1]
-            fs[g][:, :, 0:nears[g]] = jnp.zeros((CYCLES, x, nears[g], LANES), jnp.float32)
-        ex[:, :, 0:nears[2]] = jnp.zeros((CYCLES, nx, nears[2], LANES), jnp.float32)
-
-    @pl.when(jnp.logical_not(has_next))
-    def _():
-        field[:, :, slab + near:] = jnp.zeros((4, nx, near, LANES), jnp.float32)
-        for g in range(3):
-            x, rows = fs[g].shape[1:3]
-            fs[g][:, :, rows - nears[g]:] = jnp.zeros((CYCLES, x, nears[g], LANES), jnp.float32)
-        ex[:, :, slab // 2 + nears[2]:] = jnp.zeros((CYCLES, nx, nears[2], LANES), jnp.float32)
 
     def lane_of(shape):
         return iota(shape, len(shape) - 1)
@@ -605,21 +590,6 @@
         def _():
             down.wait_send()
 
-    for side in range(2):
-        absent = [jnp.logical_not((has_low, has_high)[side][axis]) for axis in range(3)]
-
-        @pl.when(absent[0])
-        def _():
-            hx[:, side] = jnp.zeros((2, ny, nz), jnp.float32)
-
-        @pl.when(absent[1])
-        def _():
-            hyr[:, side] = jnp.zeros((2, nx, 1, nz), jnp.float32)
-
-        @pl.when(absent[2])
-        def _():
-            hz[side] = jnp.zeros((ny, LANES), jnp.float32)
-
     faces = []
     for a in range(2):
         for axis in range(3 if a == 0 else 2):
@@ -633,8 +603,23 @@
                         device_id={names[axis]: place[axis] + (-1, 1)[side]}, device_id_type=MESH),
                     (has_low, has_high)[side][axis], (has_high, has_low)[side][axis]))
 
-    for f in (4, 0, 1, 2):
-        loads[f].wait()
+    every = {}
+
+    def send_out(f):
+        every[f] = spread_copies(f)
+        for c in every[f]:
+            c.start()
+        rb[f, :, me] = sb[f, mine]
+
+    loads[2].wait()
+    pack(2)
+    pl.semaphore_wait(barrier, group - 1 + jnp.where(has_low[2], 1, 0) + jnp.where(has_high[2], 1, 0))
+    send_out(2)
+    loads[0].wait()
+    pack(0)
+    send_out(0)
+    loads[1].wait()
+    loads[4].wait()
     for a in range(2):
         for side in range(2):
             row = (0, ny - 1)[side]
@@ -650,31 +635,48 @@
                     rolled = pltpu.roll(stage[v, i, :, nz - LANES:nz], to + 1, 1)
                 edge = jnp.where(tile_lane == to, rolled, edge)
         hzs[side] = edge
-    pl.semaphore_wait(barrier, group - 1 + jnp.where(has_low[2], 1, 0) + jnp.where(has_high[2], 1, 0))
     for c, goes, _ in faces:
         @pl.when(goes)
         def _():
             c.start()
 
-    every = []
-
-    def send_out(f):
-        pack(f)
-        copies = spread_copies(f)
-        for c in copies:
-            c.start()
-        every.append(copies)
-        rb[f, :, me] = sb[f, mine]
-
-    for f in range(4):
-        if f == 3:
-            loads[3].wait()
-        send_out(f)
+    pack(1)
+    send_out(1)
+    loads[3].wait()
+    pack(3)
+    send_out(3)
     loads[5].wait()
-    for c, goes, comes in faces:
-        @pl.when(comes)
-        def _():
-            c.wait_recv()
+
+    for side in range(2):
+        absent = [jnp.logical_not((has_low, has_high)[side][axis]) for axis in range(3)]
+
+        @pl.when(absent[0])
+        def _():
+            hx[:, side] = jnp.zeros((2, ny, nz), jnp.float32)
+
+        @pl.when(absent[1])
+        def _():
+            hyr[:, side] = jnp.zeros((2, nx, 1, nz), jnp.float32)
+
+        @pl.when(absent[2])
+        def _():
+            hz[side] = jnp.zeros((ny, LANES), jnp.float32)
+
+    @pl.when(jnp.logical_not(has_prev))
+    def _():
+        field[:, :, 0:near] = jnp.zeros((4, nx, near, LANES), jnp.float32)
+        for g in range(3):
+            x = fs[g].shape[1]
+            fs[g][:, :, 0:nears[g]] = jnp.zeros((CYCLES, x, nears[g], LANES), jnp.float32)
+        ex[:, :, 0:nears[2]] = jnp.zeros((CYCLES, nx, nears[2], LANES), jnp.float32)
+
+    @pl.when(jnp.logical_not(has_next))
+    def _():
+        field[:, :, slab + near:] = jnp.zeros((4, nx, near, LANES), jnp.float32)
+        for g in range(3):
+            x, rows = fs[g].shape[1:3]
+            fs[g][:, :, rows - nears[g]:] = jnp.zeros((CYCLES, x, nears[g], LANES), jnp.float32)
+        ex[:, :, slab // 2 + nears[2]:] = jnp.zeros((CYCLES, nx, nears[2], LANES), jnp.float32)
 
     tile_row = iota((ny, LANES), 0)
     count_t = nz // LANES
@@ -701,6 +703,31 @@
             (jnp.where(tile_lane == 0, ups[t], ups[t + 1]),
              jnp.where(tile_lane == LANES - 1, downs[t + 1], downs[t])) for t in range(count_t)]
 
+    def arrive(f):
+        for c in every[f]:
+            c.wait_recv()
+        for xi in range(rows_of):
+            turned = rb[f, xi].reshape((LANES, LANES)).T
+            for q in range(pieces):
+                part = turned[q * slab:(q + 1) * slab]
+                x = q * rows_of + xi
+                if f < 4:
+                    field[f, x, near:near + slab] = part
+                else:
+                    bb[x] = part
+
+    halos = {}
+
+    def take(f):
+        arrive(f)
+        halos[f] = z_copies(field.at[f], near, slab, near, zsend.at[f], zrecv.at[f])
+        z_start(halos[f])
+
+    take(2)
+    for c, goes, comes in faces:
+        @pl.when(comes)
+        def _():
+            c.wait_recv()
     for i in range(nx):
         around = [(home_shifts(4, 0, i, axis), home_shifts(axis, 1, i, axis)) for axis in range(3)]
         for t in range(count_t):
@@ -715,25 +742,8 @@
                     pulled = pulled + w * around[axis][0][t][side]
             stage[5, i, :, at] = pulled - total * stage[4, i, :, at]
 
-    def arrive(f):
-        for c in every[f]:
-            c.wait_recv()
-        for xi in range(rows_of):
-            turned = rb[f, xi].reshape((LANES, LANES)).T
-            for q in range(pieces):
-                part = turned[q * slab:(q + 1) * slab]
-                x = q * rows_of + xi
-                if f < 4:
-                    field[f, x, near:near + slab] = part
-                else:
-                    bb[x] = part
-
+    pack(4)
     send_out(4)
-    halos = []
-    for f in range(4):
-        arrive(f)
-        halos.append(z_copies(field.at[f], near, slab, near, zsend.at[f], zrecv.at[f]))
-        z_start(halos[-1])
 
     wide_rows = slab + 2 * near
     half = span // 2
@@ -758,18 +768,26 @@
         both = jnp.concatenate([rows_low.reshape((n, LANES)), rows_high.reshape((n, LANES))], 1)
         return spread(both, y_mean).reshape(rows_low.shape)
 
-    for f in range(4):
-        z_finish(halos[f])
+    def coarsen(f, low, high):
         factors = [0.25 if f == d else 1.0 for d in range(3)]
         for i in range(nx // 2):
-            cells[0][f, i] = (0.5 * factors[0]) * (
-                field[f, 2 * i] + field[f, 2 * i + 1])
-        cells[1][f] = fold_y(
-            field[f, 0:folds], field[f, folds:nx]) * factors[1]
-        coarse_rows = slab // 2 + 2 * nears[2]
+            cells[0][f, i, low:high] = (0.5 * factors[0]) * (field[f, 2 * i, low:high] + field[f, 2 * i + 1, low:high])
+        cells[1][f, :, low:high] = fold_y(field[f, 0:folds, low:high], field[f, folds:nx, low:high]) * factors[1]
+        n = (high - low) // 2
         for x in range(nx):
-            cells[2][f, x] = (0.5 * factors[2]) * (
-                field[f, x, pl.ds(0, coarse_rows, stride=2)] + field[f, x, pl.ds(1, coarse_rows, stride=2)])
+            cells[2][f, x, low // 2:high // 2] = (0.5 * factors[2]) * (
+                field[f, x, pl.ds(low, n, stride=2)] + field[f, x, pl.ds(low + 1, n, stride=2)])
+
+    def take_halo(f):
+        z_finish(halos[f])
+        coarsen(f, 0, near)
+        coarsen(f, near + slab, wide_rows)
+
+    coarsen(2, near, near + slab)
+    for f in order[1:]:
+        take(f)
+        coarsen(f, near, near + slab)
+    take_halo(2)
 
     def masks(shape, width):
         lanes = lane_of(shape)
@@ -806,6 +824,49 @@
     widths = (span, half, span)
     for g in range(3):
         count, rows = cells[g].shape[1:3]
+        at = slice(nears[g], rows - nears[g])
+        for i in range(count):
+            z_pair = [cells[g][2, i, at.start + step:at.stop + step] for step in (-1, 1)]
+            _, total = weights(lambda j, p: cells[g][j, p, at], i, count, widths[g], z_pair)
+            ms[g][6, i, at] = relaxation / total
+    own = slice(near, near + slab)
+    for i in range(nx):
+        z_pair = (field[2, i, near - 1:near + slab - 1], field[2, i, near + 1:near + slab + 1])
+        w, total = weights(lambda j, p: field[j, p, own], i, nx, span, z_pair)
+        for j in range(6):
+            fw[j, i] = w[j]
+        fw[6, i] = total
+
+    def restrict(cycle, left):
+        moves = {}
+
+        def send_first(g):
+            rows = fs[g].shape[2]
+            moves[g] = z_copies(
+                fs[g].at[cycle], nears[g], rows - 2 * nears[g], nears[g], gsend.at[cycle, g], grecv.at[cycle, g])
+            z_start(moves[g])
+
+        low2, high2 = nears[2], nears[2] + slab // 2
+        for x in range(nx):
+            first = 0.5 * (left[x, pl.ds(0, slab // 2, stride=2)] + left[x, pl.ds(1, slab // 2, stride=2)])
+            fs[2][cycle, x, low2:high2] = ms[2][6, x, low2:high2] * first
+        send_first(2)
+        for i in range(nx // 2):
+            first = 0.5 * (left[2 * i] + left[2 * i + 1])
+            fs[0][cycle, i, near:near + slab] = ms[0][6, i, near:near + slab] * first
+        send_first(0)
+        first = fold_y(left[0:folds], left[folds:nx])
+        fs[1][cycle, :, near:near + slab] = ms[1][6, :, near:near + slab] * first
+        send_first(1)
+        return moves
+
+    take_halo(0)
+    take_halo(1)
+    arrive(4)
+    first_moves = restrict(0, bb)
+    take_halo(3)
+    for g in range(3):
+        count, rows = cells[g].shape[1:3]
         for i in range(count):
             k2 = cells[g][2, i]
             z_pair = (pltpu.roll(k2, 1, 0), pltpu.roll(k2, rows - 1, 0))
@@ -815,16 +876,7 @@
             ms[g][6, i] = scale
             for j in range(6):
                 ms[g][j, i] = w[j] * scale
-    own = slice(near, near + slab)
-    for i in range(nx):
-        z_pair = (field[2, i, near - 1:near + slab - 1], field[2, i, near + 1:near + slab + 1])
-        w, total = weights(lambda j, p: field[j, p, own], i, nx, span, z_pair)
-        for j in range(6):
-            fw[j, i] = w[j]
-        fw[6, i] = total
-
-    arrive(4)
-
+    low2 = nears[2]
     pad = 8
 
     def plane(src, i, rows, shift=0):
@@ -856,8 +908,25 @@
             else:
                 dst[pad + i * rows:pad + (i + 1) * rows] = new
 
+    backs = []
+
+    def give_back(xi):
+        block = jnp.concatenate([ub[q * rows_of + xi, near:near + slab] for q in range(pieces)], 0)
+        turned = block.T
+        for j in range(group):
+            so[j, xi] = turned[j * ny:(j + 1) * ny]
+        copies = []
+        for rel in range(1, group):
+            x, y = peer(rel)
+            copies.append(pltpu.make_async_remote_copy(
+                src_ref=so.at[x * cy + y, xi], dst_ref=ro.at[mine, xi], send_sem=osend.at[rel, xi],
+                recv_sem=orecv.at[rel, xi], device_id={names[0]: x, names[1]: y}, device_id_type=MESH))
+        for c in copies:
+            c.start()
+        backs.append(copies)
+        ro[mine, xi] = so[me, xi]
+
     for cycle in range(CYCLES):
-        left = rr if cycle else bb
         for i in range(nx if cycle else 0):
             u = ub[i, near:near + slab]
             below, above = x_pair(lambda p: ub[p, near:near + slab], i, nx, span)
@@ -869,27 +938,7 @@
             residual = residual + fw[4, i] * ub[i, near - 1:near + slab - 1]
             residual = residual + fw[5, i] * ub[i, near + 1:near + slab + 1]
             rr[i] = residual
-        moves = {}
-
-        def send_first(g):
-            rows = fs[g].shape[2]
-            moves[g] = z_copies(
-                fs[g].at[cycle], nears[g], rows - 2 * nears[g], nears[g], gsend.at[cycle, g], grecv.at[cycle, g])
-            z_start(moves[g])
-
-        low2, high2 = nears[2], nears[2] + slab // 2
-        for x in range(nx):
-            first = 0.5 * (left[x, pl.ds(0, slab // 2, stride=2)] + left[x, pl.ds(1, slab // 2, stride=2)])
-            fs[2][cycle, x, low2:high2] = ms[2][6, x, low2:high2] * first
-        send_first(2)
-        for i in range(nx // 2):
-            first = 0.5 * (left[2 * i] + left[2 * i + 1])
-            fs[0][cycle, i, near:near + slab] = ms[0][6, i, near:near + slab] * first
-        send_first(0)
-        first = fold_y(left[0:folds], left[folds:nx])
-        fs[1][cycle, :, near:near + slab] = ms[1][6, :, near:near + slab] * first
-        send_first(1)
-
+        moves = first_moves if cycle == 0 else restrict(cycle, rr)
         z_finish(moves[2])
         src = fs[2].at[cycle]
         for repeat in range(nears[2] - 1):
@@ -927,20 +976,21 @@
             middle, lower, upper = (e_of[2](x, shift=step)[low // 2:low // 2 + count] for step in (0, -1, 1))
             tmp[x, pl.ds(0, count, stride=2)] = 0.75 * middle + 0.25 * lower
             tmp[x, pl.ds(1, count, stride=2)] = 0.75 * middle + 0.25 * upper
-        for i in range(nx // 2):
+        for x in range(nx) if cycle < CYCLES - 1 else [q * rows_of + xi for xi in range(rows_of) for q in range(pieces)]:
+            i, odd = x // 2, x % 2
             middle = e_of[0](i)[taken]
-            below, above = x_pair(lambda p: e_of[0](p)[taken], i, nx // 2, span)
-            if i == 0:
-                below = jnp.where(lanes >= span, below, 0.0)
-            if i == nx // 2 - 1:
-                above = jnp.where(lanes < LANES - span, above, 0.0)
-            for odd, other in ((0, below), (1, above)):
-                x = 2 * i + odd
-                from_x = 0.75 * middle + 0.25 * other
-                fold, xi = x // folds, x % folds
-                mid_y = from_y[xi * keep:(xi + 1) * keep, LANES * fold:LANES * (fold + 1)]
-                update = (from_x + mid_y) + tmp[x, 0:keep]
-                ub[x, taken] = ub[x, taken] + blending * update if cycle else blending * update
+            other = x_pair(lambda p: e_of[0](p)[taken], i, nx // 2, span)[odd]
+            if x == 0:
+                other = jnp.where(lanes >= span, other, 0.0)
+            if x == nx - 1:
+                other = jnp.where(lanes < LANES - span, other, 0.0)
+            from_x = 0.75 * middle + 0.25 * other
+            fold, xi = x // folds, x % folds
+            mid_y = from_y[xi * keep:(xi + 1) * keep, LANES * fold:LANES * (fold + 1)]
+            update = blending * ((from_x + mid_y) + tmp[x, 0:keep])
+            ub[x, taken] = ub[x, taken] + update if cycle else update
+            if cycle == CYCLES - 1 and x // rows_of == pieces - 1:
+                give_back(x % rows_of)
         if cycle < CYCLES - 1:
             @pl.when(jnp.logical_not(has_prev))
             def _():
@@ -950,29 +1000,15 @@
             def _():
                 ub[:, slab + near:] = jnp.zeros((nx, near, LANES), jnp.float32)
 
-    backs = []
     for xi in range(rows_of):
-        block = jnp.concatenate([ub[q * rows_of + xi, near:near + slab] for q in range(pieces)], 0)
-        turned = block.T
-        for j in range(group):
-            so[j, xi] = turned[j * ny:(j + 1) * ny]
-    for rel in range(1, group):
-        x, y = peer(rel)
-        backs.append(pltpu.make_async_remote_copy(
-            src_ref=so.at[x * cy + y], dst_ref=ro.at[mine], send_sem=osend.at[rel], recv_sem=orecv.at[rel],
-            device_id={names[0]: x, names[1]: y}, device_id_type=MESH))
-    for c in backs:
-        c.start()
-    ro[mine] = so[me]
-    for c in backs:
-        c.wait_recv()
-    for xi in range(rows_of):
+        for c in backs[xi]:
+            c.wait_recv()
         for t in range(nz // LANES):
             parts = regroup([ro[t * pieces + q, xi] for q in range(pieces)])
             for q in range(pieces):
                 x, at = q * rows_of + xi, slice(LANES * t, LANES * (t + 1))
                 out_ref[x, :, at] = stage[4, x, :, at] + parts[q]
-    for copies in every + [backs]:
+    for copies in list(every.values()) + backs:
         for c in copies:
             c.wait_send()
     for c, goes, _ in faces:
@@ -1025,7 +1061,7 @@
         vmem(2, 2, ny, nz), vmem(2, 2, nx, 1, nz), vmem(2, 2, nx, 1, nz), vmem(2, ny, LANES),
         vmem(2, ny, LANES), vmem(CYCLES, *shapes[2], LANES),
         dma((6,)), dma((5, group)), dma((5, group)), dma((4, 2)), dma((4, 2)),
-        dma((CYCLES, 3, 2)), dma((CYCLES, 3, 2)), dma((group,)), dma((group,)),
+        dma((CYCLES, 3, 2)), dma((CYCLES, 3, 2)), dma((group, rows_of)), dma((group, rows_of)),
         dma((2, 3, 2)), dma((2, 3, 2)), dma((CYCLES, 2)), dma((CYCLES, 2)),
     ]
     hbm = pl.BlockSpec(memory_space=pl.ANY)

time: 47.5 us -> 46.1 us (0.971)
  Pallas kernels: 45.7 us -> 44.3 us
    pallas_call x1, Pallas kernels: 45.7 us -> 44.3 us  [slab_body(): pl.pallas_call(functools.partial(slab_kernel, (nx, ny, nz), counts, names...]
where the time goes in v3:
time: 46.1 us; the launch traced here: 45.9 us
  Pallas kernels  44.3 us (96%)
  local copies, waits for them, and re-layouts  1.67 us (4%)
    pallas_call x1, Pallas kernels, slab_body(): pl.pallas_call(functools.partial(slab_kernel, (nx, ny, nz), counts, names...  44.3 us
    unnamed x1, local copies, waits for them, and re-layouts  1.67 us

profile of v3, /device:TPU:0, one launch (start us, length us, event | category | flops | bytes accessed | tf_op | source)
XLA Modules:
  0.0 45.9 jit_solution(1429502936494003033)
XLA Ops:
  0.0 44.3 %shard_map.37 = f32[16,16,256]{2,1,0:T(8,128)} custom-call(f32[16,16,256]{2,1,0:T(8,128)} %b_hbm.1, f32[4,16,16,256]{3,2,1,0:T(8,128)} %k_hbm.1, f32[16,16,256]{2,1,0:T(8,128)} %g_hbm.1), custom_call_target="tpu_custom_call" | custom-call | tf_op jit(solution)/shard_map/pallas_call | solution.py:1068
  44.3 1.7 %copy.5 = f32[16,16,256]{2,1,0:T(8,128)} copy(f32[16,16,256]{2,1,0:T(8,128)} %shard_map.37) | data formatting | bytes 524288

commit v4 on v3

--- a/solution.py
+++ b/solution.py
@@ -893,16 +893,21 @@
     def sweep(g, src, dst, inner=False):
         count, rows = fs[g].shape[1:3]
         m, f = ms[g], fs[g]
+        below = pltpu.roll(plane(src, count - 1, rows), widths[g], 1)
+        middle = plane(src, 0, rows)
         for i in range(count):
-            middle = plane(src, i, rows)
-            below, above = x_pair(lambda p: plane(src, p, rows), i, count, widths[g])
+            if i < count - 1:
+                above = follow = plane(src, i + 1, rows)
+            else:
+                above, follow = pltpu.roll(plane(src, 0, rows), LANES - widths[g], 1), None
             new = (1.0 - relaxation) * middle + f[cycle, i]
             new = new + m[0, i] * below
             new = new + m[1, i] * above
             new = new + m[2, i] * pltpu.roll(middle, 1, 1)
             new = new + m[3, i] * pltpu.roll(middle, LANES - 1, 1)
-            new = new + m[4, i] * plane(src, i, rows, -1)
-            new = new + m[5, i] * plane(src, i, rows, 1)
+            new = new + m[4, i] * pltpu.roll(middle, 1, 0)
+            new = new + m[5, i] * pltpu.roll(middle, rows - 1, 0)
+            below, middle = middle, follow
             if inner:
                 dst[i, nears[g]:rows - nears[g]] = new[nears[g]:rows - nears[g]]
             else:

time: 46.1 us -> 45.3 us (0.983)
  Pallas kernels: 44.3 us -> 43.5 us
    pallas_call x1, Pallas kernels: 44.3 us -> 43.5 us  [slab_body(): pl.pallas_call(functools.partial(slab_kernel, (nx, ny, nz), counts, names...]
where the time goes in v4:
time: 45.3 us; the launch traced here: 45.2 us
  Pallas kernels  43.5 us (96%)
  local copies, waits for them, and re-layouts  1.67 us (4%)
    pallas_call x1, Pallas kernels, slab_body(): pl.pallas_call(functools.partial(slab_kernel, (nx, ny, nz), counts, names...  43.5 us
    unnamed x1, local copies, waits for them, and re-layouts  1.67 us

profile of v4, /device:TPU:0, one launch (start us, length us, event | category | flops | bytes accessed | tf_op | source)
XLA Modules:
  0.0 45.2 jit_solution(16743286977009867779)
XLA Ops:
  0.0 43.5 %shard_map.37 = f32[16,16,256]{2,1,0:T(8,128)} custom-call(f32[16,16,256]{2,1,0:T(8,128)} %b_hbm.1, f32[4,16,16,256]{3,2,1,0:T(8,128)} %k_hbm.1, f32[16,16,256]{2,1,0:T(8,128)} %g_hbm.1), custom_call_target="tpu_custom_call" | custom-call | tf_op jit(solution)/shard_map/pallas_call | solution.py:1073
  43.5 1.7 %copy.5 = f32[16,16,256]{2,1,0:T(8,128)} copy(f32[16,16,256]{2,1,0:T(8,128)} %shard_map.37) | data formatting | bytes 524288

commit v5 on v4

--- a/solution.py
+++ b/solution.py
@@ -546,7 +546,7 @@
         for rel in range(1, group):
             x, y = peer(rel)
             copies.append(pltpu.make_async_remote_copy(
-                src_ref=sb.at[f, slab_of(x, y, gz)], dst_ref=rb.at[f, :, me],
+                src_ref=sb.at[f, slab_of(x, y, gz)], dst_ref=rb.at[f, me],
                 send_sem=send.at[f, rel], recv_sem=recv.at[f, rel],
                 device_id={names[0]: x, names[1]: y}, device_id_type=MESH))
         return copies
@@ -609,7 +609,7 @@
         every[f] = spread_copies(f)
         for c in every[f]:
             c.start()
-        rb[f, :, me] = sb[f, mine]
+        rb[f, me] = sb[f, mine]
 
     loads[2].wait()
     pack(2)
@@ -707,7 +707,7 @@
         for c in every[f]:
             c.wait_recv()
         for xi in range(rows_of):
-            turned = rb[f, xi].reshape((LANES, LANES)).T
+            turned = jnp.concatenate([rb[f, j, xi] for j in range(group)], 0).T
             for q in range(pieces):
                 part = turned[q * slab:(q + 1) * slab]
                 x = q * rows_of + xi
@@ -1050,7 +1050,7 @@
     scratch = [
         vmem(6, nx, ny, nz),
         vmem(5, *blocks),
-        vmem(5, rows_of, group, ny, LANES),
+        vmem(5, *blocks),
         vmem(4, nx, wide, LANES),
         vmem(nx, wide, LANES),
         vmem(nx, slab, LANES),

time: 45.3 us -> 45.3 us (level)
  no operation moved by 1% of the time
where the time goes in v5:
time: 45.3 us; the launch traced here: 45.2 us
  Pallas kernels  43.5 us (96%)
  local copies, waits for them, and re-layouts  1.67 us (4%)
    pallas_call x1, Pallas kernels, slab_body(): pl.pallas_call(functools.partial(slab_kernel, (nx, ny, nz), counts, names...  43.5 us
    unnamed x1, local copies, waits for them, and re-layouts  1.67 us

profile of v5, /device:TPU:0, one launch (start us, length us, event | category | flops | bytes accessed | tf_op | source)
XLA Modules:
  0.0 45.2 jit_solution(2041402525731360380)
XLA Ops:
  0.0 43.5 %shard_map.37 = f32[16,16,256]{2,1,0:T(8,128)} custom-call(f32[16,16,256]{2,1,0:T(8,128)} %b_hbm.1, f32[4,16,16,256]{3,2,1,0:T(8,128)} %k_hbm.1, f32[16,16,256]{2,1,0:T(8,128)} %g_hbm.1), custom_call_target="tpu_custom_call" | custom-call | tf_op jit(solution)/shard_map/pallas_call | solution.py:1073
  43.5 1.7 %copy.5 = f32[16,16,256]{2,1,0:T(8,128)} copy(f32[16,16,256]{2,1,0:T(8,128)} %shard_map.37) | data formatting | bytes 524288
